TPU v7x, 32 devices: a whole 2x2x4 slice. The times are simulated.
32 devices in a mesh: dom: 4 (over y, x), freq: 8 (over z, core).
Axes of the slice: x: 2, y: 2, z: 4, core: 2. Of those that a mesh axis runs over, the one named last changes fastest.
Arguments:
- voltages: float32 [512, 8192], P('freq', 'dom'), may hold values from -5 to 5
- sources: float32 [512, 8192], P('freq', 'dom'), may hold values from -20 to 20
- terminals: int32 [2, 16384], P(None, 'dom'), may hold values from 0 to 2559, as said below
- elem_current: float32 [2, 16384], P(None, 'dom'), may hold values from 0.2 to 2
- elem_charge: float32 [2, 16384], P(None, 'dom'), may hold values from 0.1 to 1
- jacobi: float32 [256, 2, 2, 8192], P('freq', None, None, 'dom'), may hold values from -1.2 to 2
Outputs:
- residual: float32 [512, 8192], P('freq', 'dom')
- newton_step: float32 [512, 8192], P('freq', 'dom')
- residual_norm: float32 [], replicated
Inputs may be any that keep to these rules, and one draw needn't show every extreme that they name: `terminals`: A terminal value below 2048 is a node of the element's own partition; a value v of 2048 or more is node (v - 2048) % 128 of partition (v - 2048) // 128, one of that partition's first 128 nodes.
All inputs are finite; a program needn't handle non-finite values.
Results may differ from a plain program's by a relative error of at most 0.0003.
Values sent between devices are 32-bit elements; how exact they have to be, the bound alone decides.
A program may use at most 64 MiB of HBM per device.

v0:
```python
import math
import jax
import jax.numpy as jnp
from jax import lax
from jax.sharding import PartitionSpec as P

S = 512
trust_radius = 2.0


def transform_table(samples):
    row_index = jnp.arange(samples, dtype=jnp.int32)
    harmonic = row_index // 2
    is_sine = row_index % 2 == 1
    column = jnp.arange(samples, dtype=jnp.int32)
    order = jnp.where(harmonic == 0, jnp.where(is_sine, samples // 2, 0), harmonic)
    phase = (order[:, None] * column[None, :] % samples).astype(jnp.float32) * (
        2.0 * math.pi / samples
    )
    use_sine = is_sine & (harmonic > 0)
    values = jnp.where(use_sine[:, None], jnp.sin(phase), jnp.cos(phase))
    weight = jnp.where(harmonic == 0, math.sqrt(1.0 / samples), math.sqrt(2.0 / samples)).astype(
        jnp.float32
    )
    forward = values * weight[:, None]
    pairs = forward.reshape(samples // 2, 2, samples)
    rate = 2.0 / samples * jnp.arange(samples // 2, dtype=jnp.float32)
    derived = jnp.stack([pairs[:, 1], -pairs[:, 0]], axis=1) * rate[:, None, None]
    return jnp.concatenate([forward, derived.reshape(samples, samples)], axis=1)


def incidence_sum(flows, terminals, column_count):
    flow_rows = flows.shape[0]
    elem_count = flows.shape[1]
    block_size = math.gcd(elem_count, 512)
    block_count = elem_count // block_size
    flow_blocks = flows.reshape(flow_rows, block_count, block_size).transpose(1, 0, 2)
    term_blocks = terminals.reshape(2, block_count, block_size).transpose(1, 0, 2)
    columns = jnp.arange(column_count, dtype=jnp.int32)

    def accumulate(total, pieces):
        flow_piece, term_piece = pieces
        plus = (term_piece[0][:, None] == columns[None, :]).astype(jnp.float32)
        minus = (term_piece[1][:, None] == columns[None, :]).astype(jnp.float32)
        signed = plus - minus
        total = total + jnp.dot(
            flow_piece, signed, precision=lax.Precision.HIGHEST, preferred_element_type=jnp.float32
        )
        return (total, None)

    start = jnp.zeros((flow_rows, column_count), jnp.float32)
    total, unused = lax.scan(accumulate, start, (flow_blocks, term_blocks))
    return total


def body(voltages, sources, terminals, elem_current, elem_charge, jacobi):
    sample_rows, node_count = voltages.shape
    freq_count = lax.axis_size("freq")
    border_count = node_count // 16
    border = lax.all_gather(voltages[:, :border_count], "dom", axis=1, tiled=True)
    extended = jnp.concatenate([voltages, border], axis=1)
    across = extended[:, terminals[0]] - extended[:, terminals[1]]
    current = elem_current[0][None, :] * across + elem_current[1][None, :] * jnp.tanh(2.0 * across)
    charge = elem_charge[0][None, :] * across + elem_charge[1][None, :] * jnp.tanh(across)
    flows = jnp.concatenate([current, charge], axis=0)
    totals = incidence_sum(flows, terminals, extended.shape[1]).reshape(
        2, sample_rows, extended.shape[1]
    )
    incoming = lax.psum_scatter(totals[:, :, node_count:], "dom", scatter_dimension=2, tiled=True)
    owned = totals[:, :, :node_count]
    owned = jnp.concatenate(
        [owned[:, :, :border_count] + incoming, owned[:, :, border_count:]], axis=2
    )
    table = transform_table(S)
    node_block = node_count // freq_count
    grouped = owned.reshape(2, sample_rows, freq_count, node_block)
    block = lax.all_to_all(grouped, "freq", split_axis=2, concat_axis=1, tiled=True)
    flat = block.reshape(2 * S, block.shape[3])
    spectra = jnp.dot(
        table, flat, precision=lax.Precision.HIGHEST, preferred_element_type=jnp.float32
    )
    transformed = lax.all_to_all(spectra, "freq", split_axis=0, concat_axis=1, tiled=True)
    residual = transformed - sources
    pairs = residual.reshape(sample_rows // 2, 2, node_count)
    raw = -(jacobi[:, :, 0, :] * pairs[:, 0:1, :] + jacobi[:, :, 1, :] * pairs[:, 1:2, :])
    raw = raw.reshape(sample_rows, node_count)
    step_squares, residual_squares = lax.psum(
        (jnp.sum(raw * raw), jnp.sum(residual * residual)), ("dom", "freq")
    )
    entry_count = S * node_count * lax.axis_size("dom")
    spread = jnp.sqrt(step_squares / entry_count + 1e-06)
    newton_step = raw * jnp.minimum(1.0, trust_radius / spread)
    residual_norm = jnp.sqrt(residual_squares)
    return (residual, newton_step, residual_norm)


def solution(mesh):
    placed = (
        P("freq", "dom"),
        P("freq", "dom"),
        P(None, "dom"),
        P(None, "dom"),
        P(None, "dom"),
        P("freq", None, None, "dom"),
    )
    return jax.shard_map(
        body,
        mesh=mesh,
        in_specs=placed,
        out_specs=(P("freq", "dom"), P("freq", "dom"), P()),
        check_vma=False,
    )
```

profile of v0, /device:TPU:12, one launch (start us, length us, event | category | flops | bytes accessed | tf_op | source)
XLA Modules:
  0.0 226.3 jit_solution(1652507804169828235)
XLA Ops:
  7.2 1.4 copy.26
  8.6 9.0 %all_gather.3 = f32[64,512]{0,1:T(8,128)S(1)} all-gather(f32[64,128]{0,1:T(8,128)S(1)} %slice.85), channel_id=1, replica_groups=mesh['dom'=4,'freq'=8] {'dom'}, dimensions={1}, use_global_device_ids=true | all-gather | bytes 163840 | tf_op jit(solution)/shard_map/all_gather | solution.py:60
  17.8 14.1 %gather_fusion = f32[4096,64]{1,0:T(8,128)} fusion(f32[64,2560]{0,1:T(8,128)S(1)} %pad_maximum_fusion, s32[4096]{0:T(1024)S(1)} %broadcast_clamp_fusion.1), kind=kCustom, calls=%fused_computation | custom fusion | bytes 2113536 | tf_op jit(solution)/shard_map/gather | solution.py:62
  31.9 14.1 %gather_fusion.1 = f32[4096,64]{1,0:T(8,128)} fusion(f32[64,2560]{0,1:T(8,128)S(1)} %pad_maximum_fusion, s32[4096]{0:T(1024)S(1)} %broadcast_clamp_fusion), kind=kCustom, calls=%fused_computation.1 | custom fusion | bytes 2113536 | tf_op jit(solution)/shard_map/gather | solution.py:62
  45.9 2.4 %sub.30 = f32[4096,64]{1,0:T(8,128)S(1)} subtract(f32[4096,64]{1,0:T(8,128)} %gather_fusion, f32[4096,64]{1,0:T(8,128)} %gather_fusion.1) | non-fusion elementwise | flops 262144 | bytes 3145728 | tf_op jit(solution)/shard_map/sub | solution.py:62
  48.4 0.6 copy.27
  49.0 0.1 copy-done.5
  49.2 0.2 slice_reduce_fusion.3
  49.4 0.3 multiply_add_fusion.1
  49.7 0.2 maximum_bitcast_fusion
  49.9 1.1 copy-done.1
  51.0 35.5 %while.12 = (s32[]{:T(128)}, f32[128,2560]{1,0:T(8,128)S(1)}, f32[8,128,512]{2,1,0:T(8,128)S(1)}, s32[8,2,512]{2,1,0:T(2,128)S(1)}, s32[]{:T(128)}, /*index=5*/s32[]{:T(128)}, s32[]{}) while((s32[]{:T(128)}, f32[128,2560]{1,0:T(8,128)S(1)}, f32[8,128,512]{2,1,0:T(8,128)S(1)}, s32[8,2,512]{2,1,0:T(2,128)S(1)}, ...), condition=%wide.region_1.2_spmd.clone.clone, body=%wide.region_0.1_spmd.clone.clone.sunk | while | flops 2020474880 | bytes 2895983 | solution.py:52
  51.0 4.4 %fusion.52 = f32[128,2560]{1,0:T(8,128)S(1)} fusion(s32[512]{0:T(512)S(1)} %bitcast.65, s32[512]{0:T(512)S(1)} %bitcast.64, f32[128,2560]{1,0:T(8,128)S(1)} %get-tuple-element.133, pred[]{:T(512)S(6)} %compare.14, f32[8,128,512]{2,1,0:T(8,128)S(1)} %get-tuple-element.141, s32[]{:T(128)} %get-tuple-element.132), kind=kOutput, calls=%fused_computation.9.clone.1 | convolution fusion | flops 2020474880 | bytes 2887685 | tf_op jit(solution)/shard_map/while/body/eval_jaxpr/dot_general | solution.py:46
  55.5 4.4 %fusion.52 = f32[128,2560]{1,0:T(8,128)S(1)} fusion(s32[512]{0:T(512)S(1)} %bitcast.65, s32[512]{0:T(512)S(1)} %bitcast.64, f32[128,2560]{1,0:T(8,128)S(1)} %get-tuple-element.133, pred[]{:T(512)S(6)} %compare.14, f32[8,128,512]{2,1,0:T(8,128)S(1)} %get-tuple-element.141, s32[]{:T(128)} %get-tuple-element.132), kind=kOutput, calls=%fused_computation.9.clone.1 | convolution fusion | flops 2020474880 | bytes 2887685 | tf_op jit(solution)/shard_map/while/body/eval_jaxpr/dot_general | solution.py:46
  59.9 4.4 %fusion.52 = f32[128,2560]{1,0:T(8,128)S(1)} fusion(s32[512]{0:T(512)S(1)} %bitcast.65, s32[512]{0:T(512)S(1)} %bitcast.64, f32[128,2560]{1,0:T(8,128)S(1)} %get-tuple-element.133, pred[]{:T(512)S(6)} %compare.14, f32[8,128,512]{2,1,0:T(8,128)S(1)} %get-tuple-element.141, s32[]{:T(128)} %get-tuple-element.132), kind=kOutput, calls=%fused_computation.9.clone.1 | convolution fusion | flops 2020474880 | bytes 2887685 | tf_op jit(solution)/shard_map/while/body/eval_jaxpr/dot_general | solution.py:46
  64.4 4.4 %fusion.52 = f32[128,2560]{1,0:T(8,128)S(1)} fusion(s32[512]{0:T(512)S(1)} %bitcast.65, s32[512]{0:T(512)S(1)} %bitcast.64, f32[128,2560]{1,0:T(8,128)S(1)} %get-tuple-element.133, pred[]{:T(512)S(6)} %compare.14, f32[8,128,512]{2,1,0:T(8,128)S(1)} %get-tuple-element.141, s32[]{:T(128)} %get-tuple-element.132), kind=kOutput, calls=%fused_computation.9.clone.1 | convolution fusion | flops 2020474880 | bytes 2887685 | tf_op jit(solution)/shard_map/while/body/eval_jaxpr/dot_general | solution.py:46
  68.8 4.4 %fusion.52 = f32[128,2560]{1,0:T(8,128)S(1)} fusion(s32[512]{0:T(512)S(1)} %bitcast.65, s32[512]{0:T(512)S(1)} %bitcast.64, f32[128,2560]{1,0:T(8,128)S(1)} %get-tuple-element.133, pred[]{:T(512)S(6)} %compare.14, f32[8,128,512]{2,1,0:T(8,128)S(1)} %get-tuple-element.141, s32[]{:T(128)} %get-tuple-element.132), kind=kOutput, calls=%fused_computation.9.clone.1 | convolution fusion | flops 2020474880 | bytes 2887685 | tf_op jit(solution)/shard_map/while/body/eval_jaxpr/dot_general | solution.py:46
  73.2 4.4 %fusion.52 = f32[128,2560]{1,0:T(8,128)S(1)} fusion(s32[512]{0:T(512)S(1)} %bitcast.65, s32[512]{0:T(512)S(1)} %bitcast.64, f32[128,2560]{1,0:T(8,128)S(1)} %get-tuple-element.133, pred[]{:T(512)S(6)} %compare.14, f32[8,128,512]{2,1,0:T(8,128)S(1)} %get-tuple-element.141, s32[]{:T(128)} %get-tuple-element.132), kind=kOutput, calls=%fused_computation.9.clone.1 | convolution fusion | flops 2020474880 | bytes 2887685 | tf_op jit(solution)/shard_map/while/body/eval_jaxpr/dot_general | solution.py:46
  77.7 4.4 %fusion.52 = f32[128,2560]{1,0:T(8,128)S(1)} fusion(s32[512]{0:T(512)S(1)} %bitcast.65, s32[512]{0:T(512)S(1)} %bitcast.64, f32[128,2560]{1,0:T(8,128)S(1)} %get-tuple-element.133, pred[]{:T(512)S(6)} %compare.14, f32[8,128,512]{2,1,0:T(8,128)S(1)} %get-tuple-element.141, s32[]{:T(128)} %get-tuple-element.132), kind=kOutput, calls=%fused_computation.9.clone.1 | convolution fusion | flops 2020474880 | bytes 2887685 | tf_op jit(solution)/shard_map/while/body/eval_jaxpr/dot_general | solution.py:46
  82.1 4.4 %fusion.52 = f32[128,2560]{1,0:T(8,128)S(1)} fusion(s32[512]{0:T(512)S(1)} %bitcast.65, s32[512]{0:T(512)S(1)} %bitcast.64, f32[128,2560]{1,0:T(8,128)S(1)} %get-tuple-element.133, pred[]{:T(512)S(6)} %compare.14, f32[8,128,512]{2,1,0:T(8,128)S(1)} %get-tuple-element.141, s32[]{:T(128)} %get-tuple-element.132), kind=kOutput, calls=%fused_computation.9.clone.1 | convolution fusion | flops 2020474880 | bytes 2887685 | tf_op jit(solution)/shard_map/while/body/eval_jaxpr/dot_general | solution.py:46
  86.5 0.7 slice.87
  87.4 0.1 fusion.34
  87.6 0.1 compare_select_fusion.3
  87.7 24.2 %reduce-scatter.2.cloned.1.call-done = f32[2,64,128]{2,1,0:T(8,128)} async-done(((f32[2,64,512]{2,1,0:T(8,128)}), f32[2,64,128]{2,1,0:T(8,128)}) %reduce-scatter.2.cloned.1.call-update) | async-done | bytes 65552 | tf_op jit(solution)/shard_map/reduce_scatter | solution.py:69
  111.9 0.9 slice_add_fusion
  112.8 0.1 pad_maximum_fusion.2
  112.9 1.1 copy.43
  114.0 5.1 %all-to-all-start = ((f32[2,64,8,256]{3,1,0,2:T(8,128)}), f32[2,64,8,256]{3,1,0,2:T(8,128)S(1)}, u32[]{:S(2)}, u32[]{:S(2)}) async-start(f32[2,64,8,256]{3,1,0,2:T(8,128)} %bitcast.38), calls=%async_computation.1 | async-start | bytes 2097152 | tf_op jit(solution)/shard_map/all_to_all | solution.py:77
  119.1 18.3 %select_multiply_fusion = f32[256,2,512]{2,1,0:T(2,128)S(1)} fusion(pred[256,2]{1,0:T(8,128)(4,1)S(1)} %fusion.34, f32[256,2]{1,0:T(8,128)S(1)} %compare_select_fusion.2, s32[256,2]{1,0:T(8,128)S(1)} %compare_select_fusion.3), kind=kLoop, calls=%fused_computation.40 | loop fusion | flops 4194304 | bytes 1053184 | tf_op jit(solution)/shard_map/mul | solution.py:25
  137.5 0.8 fusion.44
  138.3 0.9 pad_maximum_fusion.1
  139.3 1.8 stack.7
  141.2 4.3 %select_multiply_fusion.1 = f32[8,64,512]{2,1,0:T(8,128)S(1)} fusion(f32[8,64]{1,0:T(8,128)S(1)} %compare_select_fusion.6, s32[8,64]{1,0:T(8,128)S(1)} %compare_select_fusion.7, pred[8,64]{1,0:T(8,128)(4,1)S(1)} %fusion.40), kind=kLoop, calls=%fused_computation.41 | loop fusion | flops 4194304 | bytes 1053184 | tf_op jit(solution)/shard_map/mul | solution.py:25
  145.5 1.4 broadcast_multiply_fusion
  146.9 1.8 fusion.14
  148.8 17.9 %all_to_all.31 = f32[8,64,256]{2,1,0:T(8,128)S(1)} all-to-all(f32[8,64,256]{2,1,0:T(8,128)S(1)} %fusion.14), channel_id=1, replica_groups=mesh['dom'=4,'freq'=8] {'freq'}, dimensions={0} | all-to-all | bytes 1048576 | tf_op jit(solution)/shard_map/all_to_all | solution.py:82
  166.8 0.8 multiply_reduce_fusion
  167.5 0.3 reshape.233
  167.8 0.4 fusion.45
  168.4 4.3 %multiply_reduce_fusion.1 = (f32[]{:T(128)}, f32[32,2,2048]{2,1,0:T(2,128)S(1)}, f32[32,2,2048]{2,1,0:T(2,128)S(1)}) fusion(f32[32,2,2,2048]{3,2,1,0:T(2,128)S(1)} %copy-done.2, f32[32,2048]{1,0:T(8,128)S(1)} %bitcast.51, f32[32,2048]{1,0:T(8,128)S(1)} %bitcast.53), kind=kLoop, calls=%fused_computation.47 | loop fusion | flops 655359 | bytes 2621444 | tf_op jit(solution)/shard_map/reduce_sum | solution.py:88
  172.8 41.2 %all-reduce = (f32[]{:T(128)}, f32[]{:T(128)}) all-reduce(f32[]{:T(128)} %get-tuple-element.65, f32[]{:T(128)} %get-tuple-element.82), channel_id=1, replica_groups=mesh['dom'=4,'freq'=8] {'dom','freq'}, use_global_device_ids=true, to_apply=%region_4.5 | all-reduce | flops 2 | bytes 16 | tf_op jit(solution)/shard_map/psum | solution.py:87
  214.7 0.4 squeeze.23
  215.0 0.4 squeeze.24
  215.4 0.3 mul.219
  215.7 0.4 mul.220
  216.0 0.3 mul.223
  216.3 0.4 mul.224
  217.4 0.9 negate_multiply_fusion
  (45 shorter events, 0.9 us)
Async XLA Ops:
  7.2 104.8 %reduce-scatter.2.cloned.1.call-start = ((), (), s32[]{:S(2)}) async-start(), calls=%async_computation.3 | async-start | bytes 327680 | tf_op jit(solution)/shard_map/reduce_scatter | solution.py:69
  7.2 10.5 %copy-start.4 = (s32[2,4096]{1,0:T(2,128)S(1)}, s32[2,4096]{1,0:T(2,128)}, u32[]{:S(2)}) copy-start(s32[2,4096]{1,0:T(2,128)} %param.10) | copy-start | bytes 98308
  48.4 0.8 copy-start.5
  48.4 0.8 copy-start.6
  49.7 1.3 copy-start.1
  114.0 32.9 %all-to-all-start = ((f32[2,64,8,256]{3,1,0,2:T(8,128)}), f32[2,64,8,256]{3,1,0,2:T(8,128)S(1)}, u32[]{:S(2)}, u32[]{:S(2)}) async-start(f32[2,64,8,256]{3,1,0,2:T(8,128)} %bitcast.38), calls=%async_computation.1 | async-start | bytes 2097152 | tf_op jit(solution)/shard_map/all_to_all | solution.py:77
  146.9 19.8 %copy-start.3 = (f32[64,2048]{1,0:T(8,128)S(1)}, f32[64,2048]{1,0:T(8,128)}, u32[]{:S(2)}) copy-start(f32[64,2048]{1,0:T(8,128)} %param.9) | copy-start | bytes 1572868
  166.8 1.7 copy-start.2
  167.5 5.2 %copy-start = (f32[64,2048]{1,0:T(8,128)}, f32[64,2048]{1,0:T(8,128)S(1)}, u32[]{:S(2)}) copy-start(f32[64,2048]{1,0:T(8,128)S(1)} %get-tuple-element.83) | copy-start | bytes 1572868
Sparse Core Ops, SparseCore 0:
  87.4 24.4 reduce-scatter.1
where the time goes:
time: 227 us; the launch traced here: 226 us
  blocking collectives  68.1 us (30%)
  local copies, waits for them, and re-layouts  38.4 us (17%)
  matrix products  37 us (16%)
  other arithmetic  36.1 us (16%)
  waiting for transfers between devices  24.2 us (11%)
  between operations  17 us (7%)
  starting transfers between devices  5.19 us (2%)
    psum x1, blocking collectives, body(): lax.psum((jnp.sum(raw * raw), jnp.sum(residual * residual)), ('dom', 'fre...  41.2 us
    dot_general x8, matrix products, accumulate(): jnp.dot(flow_piece, signed, precision=lax.Precision.HIGHEST, preferred_el...  35.2 us
    gather x2, local copies, waits for them, and re-layouts, body(): across = extended[:, terminals[0]] - extended[:, terminals[1]]  28.2 us
    reduce_scatter x1, waiting for transfers between devices, body(): lax.psum_scatter(totals[:, :, node_count:], 'dom', scatter_dimension=2, t...  24.2 us
    mul x2, other arithmetic, transform_table(): forward = values * weight[:, None]  22.6 us
    all_to_all x1, blocking collectives, body(): lax.all_to_all(spectra, 'freq', split_axis=0, concat_axis=1, tiled=True)  17.9 us
    all_gather x1, blocking collectives, body(): lax.all_gather(voltages[:, :border_count], 'dom', axis=1, tiled=True)  8.96 us
    all_to_all x1, starting transfers between devices, body(): lax.all_to_all(grouped, 'freq', split_axis=2, concat_axis=1, tiled=True)  5.15 us
  transfers between devices with their start and end apart: 2, of which 1 were waited for; matrix products, arithmetic and copies ran while one was open for 12% of the time, Pallas kernels for 0%

commit v1 on v0

--- a/solution.py
+++ b/solution.py
@@ -6,6 +6,11 @@
 
 S = 512
 trust_radius = 2.0
+
+
+def by_each_axis(array, first, second):
+    half = lax.psum(array, first)
+    return lax.psum(half, second)
 
 
 def transform_table(samples):
@@ -84,8 +89,8 @@
     pairs = residual.reshape(sample_rows // 2, 2, node_count)
     raw = -(jacobi[:, :, 0, :] * pairs[:, 0:1, :] + jacobi[:, :, 1, :] * pairs[:, 1:2, :])
     raw = raw.reshape(sample_rows, node_count)
-    step_squares, residual_squares = lax.psum(
-        (jnp.sum(raw * raw), jnp.sum(residual * residual)), ("dom", "freq")
+    step_squares, residual_squares = by_each_axis(
+        (jnp.sum(raw * raw), jnp.sum(residual * residual)), "freq", "dom"
     )
     entry_count = S * node_count * lax.axis_size("dom")
     spread = jnp.sqrt(step_squares / entry_count + 1e-06)

time: 227 us -> 214 us (0.943)
  the two profiles are of different devices: /device:TPU:12 before, /device:TPU:0 now
where the time goes in v1:
time: 214 us; the launch traced here: 213 us
  blocking collectives  55.4 us (26%)
  local copies, waits for them, and re-layouts  38.4 us (18%)
  matrix products  37 us (17%)
  other arithmetic  36.1 us (17%)
  waiting for transfers between devices  24.4 us (11%)
  between operations  17 us (8%)
  starting transfers between devices  4.64 us (2%)
    dot_general x8, matrix products, accumulate(): jnp.dot(flow_piece, signed, precision=lax.Precision.HIGHEST, preferred_el...  35.2 us
    gather x2, local copies, waits for them, and re-layouts, body(): across = extended[:, terminals[0]] - extended[:, terminals[1]]  28.2 us
    reduce_scatter x1, waiting for transfers between devices, body(): lax.psum_scatter(totals[:, :, node_count:], 'dom', scatter_dimension=2, t...  24.4 us
    mul x2, other arithmetic, transform_table(): forward = values * weight[:, None]  22.6 us
    all_to_all x1, blocking collectives, body(): lax.all_to_all(spectra, 'freq', split_axis=0, concat_axis=1, tiled=True)  20.2 us
    psum x1, blocking collectives, by_each_axis(): half = lax.psum(array, first)  15.2 us
    all_gather x1, blocking collectives, body(): lax.all_gather(voltages[:, :border_count], 'dom', axis=1, tiled=True)  10.5 us
    psum x1, blocking collectives, by_each_axis(): return lax.psum(half, second)  9.54 us
  transfers between devices with their start and end apart: 2, of which 1 were waited for; matrix products, arithmetic and copies ran while one was open for 13% of the time, Pallas kernels for 0%

profile of v1, /device:TPU:0, one launch (start us, length us, event | category | flops | bytes accessed | tf_op | source)
XLA Modules:
  0.0 213.2 jit_solution(14607996227662126171)
XLA Ops:
  7.2 1.4 copy.26
  8.6 10.5 %all_gather.3 = f32[64,512]{0,1:T(8,128)S(1)} all-gather(f32[64,128]{0,1:T(8,128)S(1)} %slice.85), channel_id=1, replica_groups=mesh['dom'=4,'freq'=8] {'dom'}, dimensions={1}, use_global_device_ids=true | all-gather | bytes 163840 | tf_op jit(solution)/shard_map/all_gather | solution.py:65
  19.3 14.1 %gather_fusion = f32[4096,64]{1,0:T(8,128)} fusion(f32[64,2560]{0,1:T(8,128)S(1)} %pad_maximum_fusion, s32[4096]{0:T(1024)S(1)} %broadcast_clamp_fusion.1), kind=kCustom, calls=%fused_computation | custom fusion | bytes 2113536 | tf_op jit(solution)/shard_map/gather | solution.py:67
  33.4 14.1 %gather_fusion.1 = f32[4096,64]{1,0:T(8,128)} fusion(f32[64,2560]{0,1:T(8,128)S(1)} %pad_maximum_fusion, s32[4096]{0:T(1024)S(1)} %broadcast_clamp_fusion), kind=kCustom, calls=%fused_computation.1 | custom fusion | bytes 2113536 | tf_op jit(solution)/shard_map/gather | solution.py:67
  47.4 2.4 %sub.30 = f32[4096,64]{1,0:T(8,128)S(1)} subtract(f32[4096,64]{1,0:T(8,128)} %gather_fusion, f32[4096,64]{1,0:T(8,128)} %gather_fusion.1) | non-fusion elementwise | flops 262144 | bytes 3145728 | tf_op jit(solution)/shard_map/sub | solution.py:67
  49.9 0.6 copy.27
  50.5 0.1 copy-done.5
  50.7 0.2 slice_reduce_fusion.3
  50.9 0.3 multiply_add_fusion.1
  51.2 0.2 maximum_bitcast_fusion
  51.4 1.1 copy-done.1
  52.5 35.5 %while.12 = (s32[]{:T(128)}, f32[128,2560]{1,0:T(8,128)S(1)}, f32[8,128,512]{2,1,0:T(8,128)S(1)}, s32[8,2,512]{2,1,0:T(2,128)S(1)}, s32[]{:T(128)}, /*index=5*/s32[]{:T(128)}, s32[]{}) while((s32[]{:T(128)}, f32[128,2560]{1,0:T(8,128)S(1)}, f32[8,128,512]{2,1,0:T(8,128)S(1)}, s32[8,2,512]{2,1,0:T(2,128)S(1)}, ...), condition=%wide.region_1.2_spmd.clone.clone, body=%wide.region_0.1_spmd.clone.clone.sunk | while | flops 2020474880 | bytes 2895983 | solution.py:57
  52.5 4.4 %fusion.52 = f32[128,2560]{1,0:T(8,128)S(1)} fusion(s32[512]{0:T(512)S(1)} %bitcast.65, s32[512]{0:T(512)S(1)} %bitcast.64, f32[128,2560]{1,0:T(8,128)S(1)} %get-tuple-element.135, pred[]{:T(512)S(6)} %compare.14, f32[8,128,512]{2,1,0:T(8,128)S(1)} %get-tuple-element.143, s32[]{:T(128)} %get-tuple-element.134), kind=kOutput, calls=%fused_computation.9.clone.1 | convolution fusion | flops 2020474880 | bytes 2887685 | tf_op jit(solution)/shard_map/while/body/eval_jaxpr/dot_general | solution.py:51
  57.0 4.4 %fusion.52 = f32[128,2560]{1,0:T(8,128)S(1)} fusion(s32[512]{0:T(512)S(1)} %bitcast.65, s32[512]{0:T(512)S(1)} %bitcast.64, f32[128,2560]{1,0:T(8,128)S(1)} %get-tuple-element.135, pred[]{:T(512)S(6)} %compare.14, f32[8,128,512]{2,1,0:T(8,128)S(1)} %get-tuple-element.143, s32[]{:T(128)} %get-tuple-element.134), kind=kOutput, calls=%fused_computation.9.clone.1 | convolution fusion | flops 2020474880 | bytes 2887685 | tf_op jit(solution)/shard_map/while/body/eval_jaxpr/dot_general | solution.py:51
  61.4 4.4 %fusion.52 = f32[128,2560]{1,0:T(8,128)S(1)} fusion(s32[512]{0:T(512)S(1)} %bitcast.65, s32[512]{0:T(512)S(1)} %bitcast.64, f32[128,2560]{1,0:T(8,128)S(1)} %get-tuple-element.135, pred[]{:T(512)S(6)} %compare.14, f32[8,128,512]{2,1,0:T(8,128)S(1)} %get-tuple-element.143, s32[]{:T(128)} %get-tuple-element.134), kind=kOutput, calls=%fused_computation.9.clone.1 | convolution fusion | flops 2020474880 | bytes 2887685 | tf_op jit(solution)/shard_map/while/body/eval_jaxpr/dot_general | solution.py:51
  65.9 4.4 %fusion.52 = f32[128,2560]{1,0:T(8,128)S(1)} fusion(s32[512]{0:T(512)S(1)} %bitcast.65, s32[512]{0:T(512)S(1)} %bitcast.64, f32[128,2560]{1,0:T(8,128)S(1)} %get-tuple-element.135, pred[]{:T(512)S(6)} %compare.14, f32[8,128,512]{2,1,0:T(8,128)S(1)} %get-tuple-element.143, s32[]{:T(128)} %get-tuple-element.134), kind=kOutput, calls=%fused_computation.9.clone.1 | convolution fusion | flops 2020474880 | bytes 2887685 | tf_op jit(solution)/shard_map/while/body/eval_jaxpr/dot_general | solution.py:51
  70.3 4.4 %fusion.52 = f32[128,2560]{1,0:T(8,128)S(1)} fusion(s32[512]{0:T(512)S(1)} %bitcast.65, s32[512]{0:T(512)S(1)} %bitcast.64, f32[128,2560]{1,0:T(8,128)S(1)} %get-tuple-element.135, pred[]{:T(512)S(6)} %compare.14, f32[8,128,512]{2,1,0:T(8,128)S(1)} %get-tuple-element.143, s32[]{:T(128)} %get-tuple-element.134), kind=kOutput, calls=%fused_computation.9.clone.1 | convolution fusion | flops 2020474880 | bytes 2887685 | tf_op jit(solution)/shard_map/while/body/eval_jaxpr/dot_general | solution.py:51
  74.7 4.4 %fusion.52 = f32[128,2560]{1,0:T(8,128)S(1)} fusion(s32[512]{0:T(512)S(1)} %bitcast.65, s32[512]{0:T(512)S(1)} %bitcast.64, f32[128,2560]{1,0:T(8,128)S(1)} %get-tuple-element.135, pred[]{:T(512)S(6)} %compare.14, f32[8,128,512]{2,1,0:T(8,128)S(1)} %get-tuple-element.143, s32[]{:T(128)} %get-tuple-element.134), kind=kOutput, calls=%fused_computation.9.clone.1 | convolution fusion | flops 2020474880 | bytes 2887685 | tf_op jit(solution)/shard_map/while/body/eval_jaxpr/dot_general | solution.py:51
  79.2 4.4 %fusion.52 = f32[128,2560]{1,0:T(8,128)S(1)} fusion(s32[512]{0:T(512)S(1)} %bitcast.65, s32[512]{0:T(512)S(1)} %bitcast.64, f32[128,2560]{1,0:T(8,128)S(1)} %get-tuple-element.135, pred[]{:T(512)S(6)} %compare.14, f32[8,128,512]{2,1,0:T(8,128)S(1)} %get-tuple-element.143, s32[]{:T(128)} %get-tuple-element.134), kind=kOutput, calls=%fused_computation.9.clone.1 | convolution fusion | flops 2020474880 | bytes 2887685 | tf_op jit(solution)/shard_map/while/body/eval_jaxpr/dot_general | solution.py:51
  83.6 4.4 %fusion.52 = f32[128,2560]{1,0:T(8,128)S(1)} fusion(s32[512]{0:T(512)S(1)} %bitcast.65, s32[512]{0:T(512)S(1)} %bitcast.64, f32[128,2560]{1,0:T(8,128)S(1)} %get-tuple-element.135, pred[]{:T(512)S(6)} %compare.14, f32[8,128,512]{2,1,0:T(8,128)S(1)} %get-tuple-element.143, s32[]{:T(128)} %get-tuple-element.134), kind=kOutput, calls=%fused_computation.9.clone.1 | convolution fusion | flops 2020474880 | bytes 2887685 | tf_op jit(solution)/shard_map/while/body/eval_jaxpr/dot_general | solution.py:51
  88.0 0.7 slice.87
  88.9 0.1 fusion.34
  89.1 0.1 compare_select_fusion.3
  89.2 24.4 %reduce-scatter.2.cloned.1.call-done = f32[2,64,128]{2,1,0:T(8,128)} async-done(((f32[2,64,512]{2,1,0:T(8,128)}), f32[2,64,128]{2,1,0:T(8,128)}) %reduce-scatter.2.cloned.1.call-update) | async-done | bytes 65552 | tf_op jit(solution)/shard_map/reduce_scatter | solution.py:74
  113.6 0.9 slice_add_fusion
  114.5 1.1 copy.43
  115.6 4.6 %all-to-all-start = ((f32[2,64,8,256]{3,1,0,2:T(8,128)}), f32[2,64,8,256]{3,1,0,2:T(8,128)S(1)}, u32[]{:S(2)}, u32[]{:S(2)}) async-start(f32[2,64,8,256]{3,1,0,2:T(8,128)} %bitcast.38), calls=%async_computation.1 | async-start | bytes 2097152 | tf_op jit(solution)/shard_map/all_to_all | solution.py:82
  120.2 18.3 %select_multiply_fusion = f32[256,2,512]{2,1,0:T(2,128)S(1)} fusion(pred[256,2]{1,0:T(8,128)(4,1)S(1)} %fusion.34, f32[256,2]{1,0:T(8,128)S(1)} %compare_select_fusion.2, s32[256,2]{1,0:T(8,128)S(1)} %compare_select_fusion.3), kind=kLoop, calls=%fused_computation.40 | loop fusion | flops 4194304 | bytes 1053184 | tf_op jit(solution)/shard_map/mul | solution.py:30
  138.6 0.8 fusion.44
  139.4 0.9 pad_maximum_fusion.1
  140.3 1.8 stack.7
  142.3 4.3 %select_multiply_fusion.1 = f32[8,64,512]{2,1,0:T(8,128)S(1)} fusion(f32[8,64]{1,0:T(8,128)S(1)} %compare_select_fusion.6, s32[8,64]{1,0:T(8,128)S(1)} %compare_select_fusion.7, pred[8,64]{1,0:T(8,128)(4,1)S(1)} %fusion.40), kind=kLoop, calls=%fused_computation.41 | loop fusion | flops 4194304 | bytes 1053184 | tf_op jit(solution)/shard_map/mul | solution.py:30
  146.6 1.4 broadcast_multiply_fusion
  148.0 1.8 fusion.14
  149.9 20.2 %all_to_all.31 = f32[8,64,256]{2,1,0:T(8,128)S(1)} all-to-all(f32[8,64,256]{2,1,0:T(8,128)S(1)} %fusion.14), channel_id=1, replica_groups=mesh['dom'=4,'freq'=8] {'freq'}, dimensions={0} | all-to-all | bytes 1048576 | tf_op jit(solution)/shard_map/all_to_all | solution.py:87
  170.1 0.8 multiply_reduce_fusion
  170.9 0.3 reshape.233
  171.2 0.4 fusion.45
  171.8 4.3 %multiply_reduce_fusion.1 = (f32[]{:T(128)}, f32[32,2,2048]{2,1,0:T(2,128)S(1)}, f32[32,2,2048]{2,1,0:T(2,128)S(1)}) fusion(f32[32,2,2,2048]{3,2,1,0:T(2,128)S(1)} %copy-done.2, f32[32,2048]{1,0:T(8,128)S(1)} %bitcast.51, f32[32,2048]{1,0:T(8,128)S(1)} %bitcast.53), kind=kLoop, calls=%fused_computation.47 | loop fusion | flops 655359 | bytes 2621444 | tf_op jit(solution)/shard_map/reduce_sum | solution.py:93
  176.1 15.2 %all-reduce = (f32[]{:T(128)}, f32[]{:T(128)}) all-reduce(f32[]{:T(128)} %get-tuple-element.65, f32[]{:T(128)} %get-tuple-element.84), channel_id=1, replica_groups=mesh['dom'=4,'freq'=8] {'freq'}, use_global_device_ids=true, to_apply=%region_4.5 | all-reduce | flops 2 | bytes 16 | tf_op jit(solution)/shard_map/psum | solution.py:12
  191.3 9.5 %all-reduce.1 = (f32[]{:T(128)}, f32[]{:T(128)}) all-reduce(f32[]{:T(128)} %get-tuple-element.80, f32[]{:T(128)} %get-tuple-element.81), channel_id=1, replica_groups=mesh['dom'=4,'freq'=8] {'dom'}, use_global_device_ids=true, to_apply=%region_5.6 | all-reduce | flops 2 | bytes 16 | tf_op jit(solution)/shard_map/psum | solution.py:13
  201.5 0.4 squeeze.23
  201.9 0.4 squeeze.24
  202.3 0.3 mul.219
  202.6 0.4 mul.220
  202.9 0.3 mul.223
  203.2 0.4 mul.224
  204.3 0.9 negate_multiply_fusion
  (46 shorter events, 1.0 us)
Async XLA Ops:
  7.2 106.4 %reduce-scatter.2.cloned.1.call-start = ((), (), s32[]{:S(2)}) async-start(), calls=%async_computation.3 | async-start | bytes 327680 | tf_op jit(solution)/shard_map/reduce_scatter | solution.py:74
  7.2 12.0 %copy-start.4 = (s32[2,4096]{1,0:T(2,128)S(1)}, s32[2,4096]{1,0:T(2,128)}, u32[]{:S(2)}) copy-start(s32[2,4096]{1,0:T(2,128)} %param.10) | copy-start | bytes 98308
  49.9 0.8 copy-start.5
  49.9 0.8 copy-start.6
  51.2 1.3 copy-start.1
  115.6 32.3 %all-to-all-start = ((f32[2,64,8,256]{3,1,0,2:T(8,128)}), f32[2,64,8,256]{3,1,0,2:T(8,128)S(1)}, u32[]{:S(2)}, u32[]{:S(2)}) async-start(f32[2,64,8,256]{3,1,0,2:T(8,128)} %bitcast.38), calls=%async_computation.1 | async-start | bytes 2097152 | tf_op jit(solution)/shard_map/all_to_all | solution.py:82
  148.0 22.1 %copy-start.3 = (f32[64,2048]{1,0:T(8,128)S(1)}, f32[64,2048]{1,0:T(8,128)}, u32[]{:S(2)}) copy-start(f32[64,2048]{1,0:T(8,128)} %param.9) | copy-start | bytes 1572868
  170.1 1.7 copy-start.2
  170.9 5.2 %copy-start = (f32[64,2048]{1,0:T(8,128)}, f32[64,2048]{1,0:T(8,128)S(1)}, u32[]{:S(2)}) copy-start(f32[64,2048]{1,0:T(8,128)S(1)} %get-tuple-element.85) | copy-start | bytes 1572868
Sparse Core Ops, SparseCore 0:
  88.9 24.6 reduce-scatter.1
